TPU v7x, 32 devices: a whole 2x2x4 slice. The times are simulated.
32 devices in a mesh: pop: 2 (over y), ctx: 4 (over z), exp: 2 (over x), tp: 2 (over core).
Axes of the slice: x: 2, y: 2, z: 4, core: 2. Of those that a mesh axis runs over, the one named last changes fastest.
Arguments:
- tokens: bfloat16 [2048, 2688], P(('pop', 'ctx', 'tp')), parts along dimension 0, may hold values from -6 to 6
- routes: int32 [2048, 6], P(('pop', 'ctx', 'tp')), parts along dimension 0, may hold values from 0 to 15, all different within a row; in each aligned block of 128 rows (0 to 127, 128 to 255, ...) at most 64 rows name the same one
- route_gates: float32 [2048, 6], P(('pop', 'ctx', 'tp')), parts along dimension 0, may hold values from 0.05 to 1
- up_weight: bfloat16 [16, 2688, 1536], P(('ctx', 'tp'), None, 'exp'), may hold values from -0.125 to 0.125
- down_weight: bfloat16 [16, 1536, 2688], P(('ctx', 'tp'), None, 'exp'), may hold values from -0.15625 to 0.15625
- factor_seeds: int32 [32, 4], P(('pop', 'ctx', 'tp')), parts along dimension 0, may hold values from 0 to 15
- up_left: bfloat16 [16, 2688], replicated, may hold values from -0.125 to 0.125
- up_right: bfloat16 [16, 1536], P(None, 'exp'), may hold values from -3 to 3
- down_left: bfloat16 [16, 1536], replicated, may hold values from -0.15625 to 0.15625
- down_right: bfloat16 [16, 2688], P(None, 'exp'), may hold values from -3 to 3
Outputs:
- moe_output: bfloat16 [2048, 2688], P(('pop', 'ctx', 'tp'), 'exp'), parts along dimension 0
There are 2 independent parts, one for each index of `pop`. A program takes and returns all parts, laid end to end along the dimension named above; an argument that names none is the same for every part. Nothing has to cross between parts.
Inputs may be any that keep to these rules, and one draw needn't show every extreme that they name: `routes`: each row names 6 different experts. Among the 128 rows of one device (aligned blocks of 128 rows) no expert is named more than 64 times, and in every draw some expert is named exactly 64 times in some block.
All inputs are finite; a program needn't handle non-finite values.
Results may differ from a plain program's by a relative error of at most 0.0057.
Values may be sent and summed in bfloat16 or wider, within the bound.
A program may use at most 64 MiB of HBM per device.

v0:
```python
import jax
import jax.numpy as jnp
from jax import lax
from jax.sharding import PartitionSpec as P


def pick_rows(factor_table, indices):
    chooser = (
        indices[:, None] == jnp.arange(factor_table.shape[0], dtype=jnp.int32)[None, :]
    ).astype(factor_table.dtype)
    return jnp.dot(chooser, factor_table, preferred_element_type=jnp.float32).astype(
        factor_table.dtype
    )


def on_device(
    tokens,
    routes,
    route_gates,
    up_weight,
    down_weight,
    factor_seeds,
    up_left,
    up_right,
    down_left,
    down_right,
):
    dest_count = lax.axis_size("ctx") * lax.axis_size("tp")
    local_experts = up_weight.shape[0]
    experts_all = dest_count * local_experts
    tok_count, top_count = routes.shape
    capacity = 4 * tok_count * top_count // (3 * experts_all)
    model_width = tokens.shape[1]
    flat_routes = routes.reshape(-1)
    chooser = (flat_routes[:, None] == jnp.arange(experts_all, dtype=jnp.int32)[None, :]).astype(
        jnp.int32
    )
    earlier = jnp.cumsum(chooser, axis=0) - chooser
    slot_index = jnp.sum(earlier * chooser, axis=1)
    target = flat_routes * capacity + slot_index
    pair_token = jnp.arange(tok_count * top_count, dtype=jnp.int32) // top_count + 1
    owner_token = jnp.zeros((experts_all * capacity,), jnp.int32).at[target].set(pair_token)
    source_row = jnp.where(owner_token > 0, owner_token - 1, tok_count)
    padded_tokens = jnp.concatenate([tokens, jnp.zeros((1, model_width), tokens.dtype)], axis=0)
    token_rows = padded_tokens[source_row]
    outgoing = token_rows.reshape(dest_count, local_experts, capacity, model_width)
    left_up = pick_rows(up_left, factor_seeds[:, 0])
    right_up = pick_rows(up_right, factor_seeds[:, 1])
    left_down = pick_rows(down_left, factor_seeds[:, 2])
    right_down = pick_rows(down_right, factor_seeds[:, 3])
    buffer = lax.all_to_all(outgoing, ("ctx", "tp"), split_axis=0, concat_axis=0, tiled=True)
    up_act = jnp.einsum("slcd,ldh->slch", buffer, up_weight, preferred_element_type=jnp.float32)
    low_rank = jnp.einsum("slcd,ld->slc", buffer, left_up, preferred_element_type=jnp.float32)
    up_act = up_act + low_rank[..., None] * right_up[None, :, None, :].astype(jnp.float32)
    hidden = (jnp.maximum(up_act, 0.0) ** 2).astype(jnp.bfloat16)
    full_hidden = lax.all_gather(hidden, "exp", axis=3, tiled=True)
    summed = jnp.einsum(
        "slch,lhd->slcd", full_hidden, down_weight, preferred_element_type=jnp.float32
    )
    rank_sum = jnp.einsum(
        "slch,lh->slc", full_hidden, left_down, preferred_element_type=jnp.float32
    )
    result = (
        summed + rank_sum[..., None] * right_down[None, :, None, :].astype(jnp.float32)
    ).astype(jnp.bfloat16)
    returned = lax.all_to_all(result, ("ctx", "tp"), split_axis=0, concat_axis=0, tiled=True)
    back_rows = returned.reshape(experts_all * capacity, -1)
    picked = back_rows[target]
    normed = (route_gates / jnp.sum(route_gates, axis=1, keepdims=True)).reshape(-1)
    weighted = picked.astype(jnp.float32) * normed[:, None]
    moe_output = jnp.sum(weighted.reshape(tok_count, top_count, -1), axis=1)
    return moe_output.astype(jnp.bfloat16)


def solution(mesh):
    in_specs = (
        P(("pop", "ctx", "tp"), None),
        P(("pop", "ctx", "tp"), None),
        P(("pop", "ctx", "tp"), None),
        P(("ctx", "tp"), None, "exp"),
        P(("ctx", "tp"), None, "exp"),
        P(("pop", "ctx", "tp"), None),
        P(),
        P(None, "exp"),
        P(),
        P(None, "exp"),
    )
    out_specs = P(("pop", "ctx", "tp"), "exp")
    return jax.shard_map(
        on_device, mesh=mesh, in_specs=in_specs, out_specs=out_specs, check_vma=False
    )
```

profile of v0, /device:TPU:0, one launch (start us, length us, event | category | flops | bytes accessed | tf_op | source)
XLA Modules:
  0.0 316.2 jit_solution(15399134807292461094)
XLA Ops:
  6.5 0.0 copy-start
  6.5 0.8 copy.28
  7.4 0.1 eq.89
  7.5 0.1 eq.85
  7.6 0.7 broadcast_multiply_fusion
  8.4 1.7 reduce-window.6
  10.1 0.3 slice_reduce_fusion
  10.4 0.1 copy.27
  10.5 0.1 mul.56
  10.6 0.1 fusion.23
  10.7 3.4 %scatter_custom_fusion = s32[1024]{0:T(1024)S(1)} fusion(s32[768]{0:T(1024)S(1)} %fusion.33, s32[768]{0:T(1024)S(1)} %fusion.28, s32[]{:T(128)} %constant.11.clone.1), kind=kCustom, calls=%fused_computation.52 | custom fusion | bytes 4100 | tf_op jit(solution)/shard_map/scatter | solution.py:42
  14.1 1.2 concatenate.3
  15.3 6.6 %gather_fusion = bf16[1024,2688]{1,0:T(8,128)(2,1)} fusion(bf16[129,2688]{1,0:T(8,128)(2,1)S(1)} %concatenate.3, s32[1024]{0:T(1024)S(1)} %fusion.31), kind=kCustom, calls=%fused_computation | custom fusion | bytes 11014144 | tf_op jit(solution)/shard_map/gather | solution.py:45
  21.9 0.0 copy-start.2
  21.9 0.0 copy-start.5
  21.9 6.5 %all-to-all-start = ((bf16[8,2,64,2688]{3,2,1,0:T(8,128)(2,1)}), bf16[8,2,64,2688]{3,2,1,0:T(8,128)(2,1)}, u32[]{:S(2)}, u32[]{:S(2)}) async-start(bf16[8,2,64,2688]{3,2,1,0:T(8,128)(2,1)} %bitcast.67), calls=%async_computation | async-start | bytes 11010048 | tf_op jit(solution)/shard_map/all_to_all | solution.py:51
  28.4 0.0 all-gather.2.cloned.1.call-start
  28.4 0.0 copy-done.2
  28.4 0.2 slice_reduce_fusion.2
  28.6 0.0 copy-done
  28.7 0.2 fusion.10
  28.9 0.0 copy-done.5
  28.9 0.2 fusion.20
  29.1 121.5 %all-to-all-done = bf16[8,2,64,2688]{3,2,1,0:T(8,128)(2,1)} async-done(((bf16[8,2,64,2688]{3,2,1,0:T(8,128)(2,1)}), bf16[8,2,64,2688]{3,2,1,0:T(8,128)(2,1)}, u32[]{:S(2)}, u32[]{:S(2)}) %all-to-all-start) | async-done | bytes 5505056 | tf_op jit(solution)/shard_map/all_to_all | solution.py:51
  150.5 4.9 %fusion.5 = f32[2,1,8,64]{3,1,2,0:T(1,128)S(1)} fusion(bf16[8,2,64,2688]{3,2,1,0:T(8,128)(2,1)} %all-to-all-done, bf16[2,2688,1,1]{1,0,2,3:T(2,128)(2,1)S(1)} %fusion.10), kind=kOutput, calls=%fused_computation.10 | convolution fusion | flops 5505024 | bytes 5519872 | tf_op jit(solution)/shard_map/slcd,ld->slc/dot_general | solution.py:53
  155.4 0.0 copy-start.3
  155.4 0.0 copy-start.4
  155.4 10.8 %fusion.13 = bf16[8,2,64,768]{3,2,0,1:T(8,128)(2,1)} fusion(bf16[2,2688,768]{2,1,0:T(8,128)(2,1)} %param.13, bf16[8,2,64,2688]{3,2,1,0:T(8,128)(2,1)} %all-to-all-done, f32[2,768]{1,0:T(2,128)S(1)} %fusion.20, f32[8,2,64]{2,0,1:T(8,128)S(1)} %bitcast.70), kind=kOutput, calls=%fused_computation.18 | convolution fusion | flops 4231790592 | bytes 15345664 | tf_op jit(solution)/shard_map/slcd,ldh->slch/dot_general | solution.py:52
  166.3 0.0 all-gather.2.cloned.1.call-update
  166.3 0.0 copy-done.3
  166.3 0.2 fusion.15
  166.5 0.0 copy-done.4
  166.5 0.2 fusion.14
  166.7 43.6 %all-gather.2.cloned.1.call-done = bf16[8,2,64,1536]{3,2,0,1:T(8,128)(2,1)} async-done(((bf16[8,2,64,768]{3,2,0,1:T(8,128)(2,1)}), bf16[8,2,64,1536]{3,2,0,1:T(8,128)(2,1)}) %all-gather.2.cloned.1.call-update) | async-done | bytes 3145744 | tf_op jit(solution)/shard_map/all_gather | solution.py:56
  210.3 3.2 %fusion.26 = f32[2,1,8,64]{3,1,2,0:T(1,128)S(1)} fusion(bf16[8,2,64,1536]{3,2,0,1:T(8,128)(2,1)} %all-gather.2.cloned.1.call-done, bf16[2,1536,1,1]{1,0,2,3:T(2,128)(2,1)S(1)} %fusion.15), kind=kOutput, calls=%fused_computation.36 | convolution fusion | flops 3145728 | bytes 3155968 | tf_op jit(solution)/shard_map/slch,lh->slc/dot_general | solution.py:60
  213.5 9.2 %fusion.4 = bf16[8,2,64,1344]{3,2,0,1:T(8,128)(2,1)S(1)} fusion(bf16[8,2,64,1536]{3,2,0,1:T(8,128)(2,1)} %all-gather.2.cloned.1.call-done, bf16[2,1536,1344]{1,2,0:T(8,128)(2,1)} %param.14, f32[2,1344]{1,0:T(2,128)S(1)} %fusion.14, f32[8,2,64]{2,0,1:T(8,128)S(1)} %bitcast.69), kind=kOutput, calls=%fused_computation.8 | convolution fusion | flops 4231987200 | bytes 14170624 | tf_op jit(solution)/shard_map/slch,lhd->slcd/dot_general | solution.py:57
  222.7 0.0 copy-start.1
  222.7 1.8 copy.32
  224.5 4.6 %all-to-all-start.1 = ((bf16[8,2,64,1344]{3,2,1,0:T(8,128)(2,1)}), bf16[8,2,64,1344]{3,2,1,0:T(8,128)(2,1)S(1)}, u32[]{:S(2)}, u32[]{:S(2)}) async-start(bf16[8,2,64,1344]{3,2,1,0:T(8,128)(2,1)} %copy.32), calls=%async_computation.1 | async-start | bytes 5767168 | tf_op jit(solution)/shard_map/all_to_all | solution.py:66
  229.1 0.0 copy-done.1
  229.1 0.1 copy.33
  229.3 65.7 %all-to-all-done.1 = bf16[8,2,64,1344]{3,2,1,0:T(8,128)(2,1)S(1)} async-done(((bf16[8,2,64,1344]{3,2,1,0:T(8,128)(2,1)}), bf16[8,2,64,1344]{3,2,1,0:T(8,128)(2,1)S(1)}, u32[]{:S(2)}, u32[]{:S(2)}) %all-to-all-start.1) | async-done | bytes 2752544 | tf_op jit(solution)/shard_map/all_to_all | solution.py:66
  295.0 3.7 %gather_fusion.1 = bf16[768,1344]{1,0:T(8,128)(2,1)} fusion(bf16[1024,1344]{1,0:T(8,128)(2,1)S(1)} %bitcast.66, s32[1024]{0:T(1024)S(1)} %pad_clamp_fusion), kind=kCustom, calls=%fused_computation.1 | custom fusion | bytes 4131840 | tf_op jit(solution)/shard_map/gather | solution.py:68
  298.7 5.0 %reshape.72 = f32[128,6,1344]{2,1,0:T(8,128)} reshape(bf16[768,1344]{1,0:T(8,128)(2,1)} %gather_fusion.1) | data formatting | bytes 6193152 | tf_op jit(solution)/shard_map/convert_element_type | solution.py:70
  303.7 4.7 %multiply_reduce_fusion = bf16[128,1344]{1,0:T(8,128)(2,1)S(1)} fusion(f32[128,6,1344]{2,1,0:T(8,128)} %reshape.72, f32[128,6]{1,0:T(8,128)S(1)} %copy.33), kind=kLoop, calls=%fused_computation.9 | loop fusion | flops 1892352 | bytes 4475904 | tf_op jit(solution)/shard_map/reduce_sum | solution.py:71
  308.5 0.9 copy.34
  (8 shorter events, 0.1 us)
Async XLA Ops:
  6.5 22.1 %copy-start = (bf16[16,2688]{1,0:T(8,128)(2,1)S(1)}, bf16[16,2688]{1,0:T(8,128)(2,1)}, u32[]{:S(2)}) copy-start(bf16[16,2688]{1,0:T(8,128)(2,1)} %param.16) | copy-start | bytes 258052
  21.9 6.5 %copy-start.2 = (s32[2,4]{1,0:T(2,128)S(1)}, s32[2,4]{1,0:T(2,128)}, u32[]{:S(2)}) copy-start(s32[2,4]{1,0:T(2,128)} %param.15) | copy-start | bytes 100
  21.9 7.0 %copy-start.5 = (bf16[16,768]{1,0:T(8,128)(2,1)S(1)}, bf16[16,768]{1,0:T(8,128)(2,1)}, u32[]{:S(2)}) copy-start(bf16[16,768]{1,0:T(8,128)(2,1)} %param.17) | copy-start | bytes 73732
  21.9 128.7 %all-to-all-start = ((bf16[8,2,64,2688]{3,2,1,0:T(8,128)(2,1)}), bf16[8,2,64,2688]{3,2,1,0:T(8,128)(2,1)}, u32[]{:S(2)}, u32[]{:S(2)}) async-start(bf16[8,2,64,2688]{3,2,1,0:T(8,128)(2,1)} %bitcast.67), calls=%async_computation | async-start | bytes 11010048 | tf_op jit(solution)/shard_map/all_to_all | solution.py:51
  28.4 181.9 %all-gather.2.cloned.1.call-start = ((), (), s32[]{:S(2)}) async-start(), calls=%async_computation.2 | async-start | bytes 4718592 | tf_op jit(solution)/shard_map/all_gather | solution.py:56
  155.4 10.9 %copy-start.3 = (bf16[16,1536]{1,0:T(8,128)(2,1)S(1)}, bf16[16,1536]{1,0:T(8,128)(2,1)}, u32[]{:S(2)}) copy-start(bf16[16,1536]{1,0:T(8,128)(2,1)} %param.18) | copy-start | bytes 147460
  155.4 11.1 %copy-start.4 = (bf16[16,1344]{1,0:T(8,128)(2,1)S(1)}, bf16[16,1344]{1,0:T(8,128)(2,1)}, u32[]{:S(2)}) copy-start(bf16[16,1344]{1,0:T(8,128)(2,1)} %param.19) | copy-start | bytes 129028
  222.7 6.4 %copy-start.1 = (f32[128,6]{0,1:T(8,128)S(1)}, f32[128,6]{0,1:T(8,128)}, u32[]{:S(2)}) copy-start(f32[128,6]{0,1:T(8,128)} %param.12) | copy-start | bytes 9220
  224.5 70.5 %all-to-all-start.1 = ((bf16[8,2,64,1344]{3,2,1,0:T(8,128)(2,1)}), bf16[8,2,64,1344]{3,2,1,0:T(8,128)(2,1)S(1)}, u32[]{:S(2)}, u32[]{:S(2)}) async-start(bf16[8,2,64,1344]{3,2,1,0:T(8,128)(2,1)} %copy.32), calls=%async_computation.1 | async-start | bytes 5767168 | tf_op jit(solution)/shard_map/all_to_all | solution.py:66
Sparse Core Ops, SparseCore 0:
  166.4 43.8 all-gather.1
where the time goes:
time: 317 us; the launch traced here: 316 us
  waiting for transfers between devices  231 us (73%)
  matrix products  28.9 us (9%)
  local copies, waits for them, and re-layouts  24.5 us (8%)
  between operations  13.5 us (4%)
  starting transfers between devices  11.1 us (4%)
  other arithmetic  7.34 us (2%)
    all_to_all x1, waiting for transfers between devices, on_device(): lax.all_to_all(outgoing, ('ctx', 'tp'), split_axis=0, concat_axis=0, tile...  121 us
    all_to_all x1, waiting for transfers between devices, on_device(): lax.all_to_all(result, ('ctx', 'tp'), split_axis=0, concat_axis=0, tiled=...  65.7 us
    all_gather x1, waiting for transfers between devices, on_device(): full_hidden = lax.all_gather(hidden, 'exp', axis=3, tiled=True)  43.6 us
    dot_general x1, matrix products, on_device(): jnp.einsum('slcd,ldh->slch', buffer, up_weight, preferred_element_type=jn...  10.8 us
    dot_general x1, matrix products, on_device(): jnp.einsum('slch,lhd->slcd', full_hidden, down_weight, preferred_element_...  9.17 us
    gather x1, local copies, waits for them, and re-layouts, on_device(): token_rows = padded_tokens[source_row]  6.58 us
    all_to_all x1, starting transfers between devices, on_device(): lax.all_to_all(outgoing, ('ctx', 'tp'), split_axis=0, concat_axis=0, tile...  6.49 us
  transfers between devices with their start and end apart: 3, of which 3 were waited for; matrix products, arithmetic and copies ran while one was open for 0% of the time, Pallas kernels for 0%

commit v1 on v0

--- a/solution.py
+++ b/solution.py
@@ -53,7 +53,9 @@
     low_rank = jnp.einsum("slcd,ld->slc", buffer, left_up, preferred_element_type=jnp.float32)
     up_act = up_act + low_rank[..., None] * right_up[None, :, None, :].astype(jnp.float32)
     hidden = (jnp.maximum(up_act, 0.0) ** 2).astype(jnp.bfloat16)
-    full_hidden = lax.all_gather(hidden, "exp", axis=3, tiled=True)
+    full_hidden = jnp.concatenate(
+        lax.all_to_all(jnp.stack([hidden] * lax.axis_size("exp")), "exp", 0, 0), axis=3
+    )
     summed = jnp.einsum(
         "slch,lhd->slcd", full_hidden, down_weight, preferred_element_type=jnp.float32
     )

time: 317 us -> 297 us (0.937)
  between operations: 13.5 us -> 0.17 us
  waiting for transfers between devices: 231 us -> 223 us
  matrix products: 28.9 us -> 25.3 us
  starting transfers between devices: 11.1 us -> 14.5 us
    all_gather x1 -> x0, waiting for transfers between devices: 43.6 us -> none  [on_device(): full_hidden = lax.all_gather(hidden, 'exp', axis=3, tiled=True)]
    all_to_all x0 -> x1, waiting for transfers between devices: none -> 35.6 us  [on_device(): lax.all_to_all(jnp.stack([hidden] * lax.axis_size('exp')), 'exp', 0, 0)]
    all_to_all x0 -> x1, starting transfers between devices: none -> 4.08 us  [on_device(): lax.all_to_all(jnp.stack([hidden] * lax.axis_size('exp')), 'exp', 0, 0)]
where the time goes in v1:
time: 297 us
  waiting for transfers between devices  223 us (75%)
  matrix products  25.3 us (9%)
  local copies, waits for them, and re-layouts  24.8 us (8%)
  starting transfers between devices  14.5 us (5%)
  other arithmetic  9.28 us (3%)
    all_to_all x1, waiting for transfers between devices, on_device(): lax.all_to_all(outgoing, ('ctx', 'tp'), split_axis=0, concat_axis=0, tile...  122 us
    all_to_all x1, waiting for transfers between devices, on_device(): lax.all_to_all(result, ('ctx', 'tp'), split_axis=0, concat_axis=0, tiled=...  65.5 us
    all_to_all x1, waiting for transfers between devices, on_device(): lax.all_to_all(jnp.stack([hidden] * lax.axis_size('exp')), 'exp', 0, 0)  35.6 us
    dot_general x1, matrix products, on_device(): jnp.einsum('slcd,ldh->slch', buffer, up_weight, preferred_element_type=jn...  9.66 us
    dot_general x1, matrix products, on_device(): jnp.einsum('slch,lhd->slcd', full_hidden, down_weight, preferred_element_...  8.67 us
    gather x1, local copies, waits for them, and re-layouts, on_device(): token_rows = padded_tokens[source_row]  6.58 us
    all_to_all x1, starting transfers between devices, on_device(): lax.all_to_all(outgoing, ('ctx', 'tp'), split_axis=0, concat_axis=0, tile...  6.49 us
  transfers between devices with their start and end apart: 3, of which 3 were waited for; matrix products, arithmetic and copies ran while one was open for 0% of the time, Pallas kernels for 0%

profile of v1, /device:TPU:0, one launch (start us, length us, event | category | flops | bytes accessed | tf_op | source)
XLA Modules:
  0.0 296.7 jit_solution(13548926594514431275)
XLA Ops:
  0.0 0.0 copy-start
  0.0 0.8 copy.32
  0.8 0.1 eq.89
  1.0 0.1 eq.85
  1.1 0.7 broadcast_multiply_fusion
  1.8 1.7 reduce-window.6
  3.5 0.3 slice_reduce_fusion
  3.8 0.1 copy.31
  3.9 0.1 mul.56
  4.1 0.1 fusion.28
  4.2 3.4 %scatter_custom_fusion = s32[1024]{0:T(1024)S(1)} fusion(s32[768]{0:T(1024)S(1)} %fusion.38, s32[768]{0:T(1024)S(1)} %fusion.33, s32[]{:T(128)} %constant.11.clone.1), kind=kCustom, calls=%fused_computation.54 | custom fusion | bytes 4100 | tf_op jit(solution)/shard_map/scatter | solution.py:42
  7.6 1.2 concatenate.3
  8.8 6.6 %gather_fusion = bf16[1024,2688]{1,0:T(8,128)(2,1)} fusion(bf16[129,2688]{1,0:T(8,128)(2,1)S(1)} %concatenate.3, s32[1024]{0:T(1024)S(1)} %fusion.36), kind=kCustom, calls=%fused_computation | custom fusion | bytes 11014144 | tf_op jit(solution)/shard_map/gather | solution.py:45
  15.3 0.0 copy-start.2
  15.3 0.0 copy-start.5
  15.3 6.5 %all-to-all-start = ((bf16[8,2,64,2688]{3,2,1,0:T(8,128)(2,1)}), bf16[8,2,64,2688]{3,2,1,0:T(8,128)(2,1)}, u32[]{:S(2)}, u32[]{:S(2)}) async-start(bf16[8,2,64,2688]{3,2,1,0:T(8,128)(2,1)} %bitcast.76), calls=%async_computation | async-start | bytes 11010048 | tf_op jit(solution)/shard_map/all_to_all | solution.py:51
  21.8 0.0 copy-done.2
  21.8 0.2 slice_reduce_fusion.2
  22.1 0.0 copy-done
  22.1 0.2 fusion.10
  22.3 0.0 copy-done.5
  22.3 0.2 fusion.25
  22.5 121.5 %all-to-all-done = bf16[8,2,64,2688]{3,2,1,0:T(8,128)(2,1)} async-done(((bf16[8,2,64,2688]{3,2,1,0:T(8,128)(2,1)}), bf16[8,2,64,2688]{3,2,1,0:T(8,128)(2,1)}, u32[]{:S(2)}, u32[]{:S(2)}) %all-to-all-start) | async-done | bytes 5505056 | tf_op jit(solution)/shard_map/all_to_all | solution.py:51
  144.0 4.9 %fusion.5 = f32[2,1,8,64]{3,1,2,0:T(1,128)S(1)} fusion(bf16[8,2,64,2688]{3,2,1,0:T(8,128)(2,1)} %all-to-all-done, bf16[2,2688,1,1]{1,0,2,3:T(2,128)(2,1)S(1)} %fusion.10), kind=kOutput, calls=%fused_computation.10 | convolution fusion | flops 5505024 | bytes 5519872 | tf_op jit(solution)/shard_map/slcd,ld->slc/dot_general | solution.py:53
  148.9 9.7 %fusion.20 = bf16[1,8,2,64,768]{4,3,1,2,0:T(8,128)(2,1)S(1)} fusion(f32[2,768]{1,0:T(2,128)S(1)} %fusion.25, f32[8,2,64]{2,0,1:T(8,128)S(1)} %bitcast.82, bf16[2,2688,768]{2,1,0:T(8,128)(2,1)} %param.13, bf16[8,2,64,2688]{3,2,1,0:T(8,128)(2,1)} %all-to-all-done), kind=kOutput, calls=%fused_computation.24 | convolution fusion | flops 4231790592 | bytes 15345664 | tf_op jit(solution)/shard_map/slcd,ldh->slch/dot_general | solution.py:52
  158.6 1.9 pad_maximum_fusion
  160.5 0.0 copy-start.3
  160.5 0.0 copy-start.4
  160.5 4.1 %all-to-all-start.1 = ((bf16[2,8,2,64,768]{4,3,1,2,0:T(8,128)(2,1)}), bf16[2,8,2,64,768]{4,3,1,2,0:T(8,128)(2,1)S(1)}, u32[]{:S(2)}, u32[]{:S(2)}) async-start(bf16[2,8,2,64,768]{4,3,1,2,0:T(8,128)(2,1)} %pad_maximum_fusion), calls=%async_computation.1 | async-start | bytes 6291456 | tf_op jit(solution)/shard_map/all_to_all | solution.py:57
  164.6 0.0 copy-done.3
  164.6 0.2 fusion.15
  164.8 0.0 copy-done.4
  164.8 0.2 fusion.14
  165.0 35.6 %all-to-all-done.1 = bf16[2,8,2,64,768]{4,3,1,2,0:T(8,128)(2,1)S(1)} async-done(((bf16[2,8,2,64,768]{4,3,1,2,0:T(8,128)(2,1)}), bf16[2,8,2,64,768]{4,3,1,2,0:T(8,128)(2,1)S(1)}, u32[]{:S(2)}, u32[]{:S(2)}) %all-to-all-start.1) | async-done | bytes 3145760 | tf_op jit(solution)/shard_map/all_to_all | solution.py:57
  200.6 0.3 copy.50
  200.9 1.3 fusion.31
  202.2 8.7 %fusion.4 = bf16[8,2,64,1344]{3,2,0,1:T(8,128)(2,1)S(1)} fusion(bf16[8,2,64,1536]{3,2,0,1:T(8,128)(2,1)S(1)} %bitcast.79, bf16[2,1536,1344]{1,2,0:T(8,128)(2,1)} %param.14, f32[2,1344]{1,0:T(2,128)S(1)} %fusion.14, f32[8,2,64]{2,0,1:T(8,128)S(1)} %bitcast.81), kind=kOutput, calls=%fused_computation.8 | convolution fusion | flops 4231987200 | bytes 14170624 | tf_op jit(solution)/shard_map/slch,lhd->slcd/dot_general | solution.py:59
  210.9 1.8 copy.38
  212.7 0.0 copy-start.1
  212.7 3.9 %all-to-all-start.2 = ((bf16[8,2,64,1344]{3,2,1,0:T(8,128)(2,1)}), bf16[8,2,64,1344]{3,2,1,0:T(8,128)(2,1)S(1)}, u32[]{:S(2)}, u32[]{:S(2)}) async-start(bf16[8,2,64,1344]{3,2,1,0:T(8,128)(2,1)} %copy.38), calls=%async_computation.2 | async-start | bytes 5767168 | tf_op jit(solution)/shard_map/all_to_all | solution.py:68
  216.7 0.0 copy-done.1
  216.7 0.1 copy.39
  216.8 65.5 %all-to-all-done.2 = bf16[8,2,64,1344]{3,2,1,0:T(8,128)(2,1)S(1)} async-done(((bf16[8,2,64,1344]{3,2,1,0:T(8,128)(2,1)}), bf16[8,2,64,1344]{3,2,1,0:T(8,128)(2,1)S(1)}, u32[]{:S(2)}, u32[]{:S(2)}) %all-to-all-start.2) | async-done | bytes 2752544 | tf_op jit(solution)/shard_map/all_to_all | solution.py:68
  282.3 3.7 %gather_fusion.1 = bf16[768,1344]{1,0:T(8,128)(2,1)} fusion(bf16[1024,1344]{1,0:T(8,128)(2,1)S(1)} %bitcast.75, s32[1024]{0:T(1024)S(1)} %pad_clamp_fusion), kind=kCustom, calls=%fused_computation.1 | custom fusion | bytes 4131840 | tf_op jit(solution)/shard_map/gather | solution.py:70
  286.0 5.0 %reshape.80 = f32[128,6,1344]{2,1,0:T(8,128)} reshape(bf16[768,1344]{1,0:T(8,128)(2,1)} %gather_fusion.1) | data formatting | bytes 6193152 | tf_op jit(solution)/shard_map/convert_element_type | solution.py:72
  291.0 4.7 %multiply_reduce_fusion = bf16[128,1344]{1,0:T(8,128)(2,1)S(1)} fusion(f32[128,6,1344]{2,1,0:T(8,128)} %reshape.80, f32[128,6]{1,0:T(8,128)S(1)} %copy.39), kind=kLoop, calls=%fused_computation.9 | loop fusion | flops 1892352 | bytes 4475904 | tf_op jit(solution)/shard_map/reduce_sum | solution.py:73
  295.8 0.9 copy.40
  (8 shorter events, 0.1 us)
Async XLA Ops:
  0.0 22.1 %copy-start = (bf16[16,2688]{1,0:T(8,128)(2,1)S(1)}, bf16[16,2688]{1,0:T(8,128)(2,1)}, u32[]{:S(2)}) copy-start(bf16[16,2688]{1,0:T(8,128)(2,1)} %param.16) | copy-start | bytes 258052
  15.3 6.5 %copy-start.2 = (s32[2,4]{1,0:T(2,128)S(1)}, s32[2,4]{1,0:T(2,128)}, u32[]{:S(2)}) copy-start(s32[2,4]{1,0:T(2,128)} %param.15) | copy-start | bytes 100
  15.3 6.9 %copy-start.5 = (bf16[16,768]{1,0:T(8,128)(2,1)S(1)}, bf16[16,768]{1,0:T(8,128)(2,1)}, u32[]{:S(2)}) copy-start(bf16[16,768]{1,0:T(8,128)(2,1)} %param.17) | copy-start | bytes 73732
  15.3 128.7 %all-to-all-start = ((bf16[8,2,64,2688]{3,2,1,0:T(8,128)(2,1)}), bf16[8,2,64,2688]{3,2,1,0:T(8,128)(2,1)}, u32[]{:S(2)}, u32[]{:S(2)}) async-start(bf16[8,2,64,2688]{3,2,1,0:T(8,128)(2,1)} %bitcast.76), calls=%async_computation | async-start | bytes 11010048 | tf_op jit(solution)/shard_map/all_to_all | solution.py:51
  160.5 4.1 %copy-start.3 = (bf16[16,1536]{1,0:T(8,128)(2,1)S(1)}, bf16[16,1536]{1,0:T(8,128)(2,1)}, u32[]{:S(2)}) copy-start(bf16[16,1536]{1,0:T(8,128)(2,1)} %param.18) | copy-start | bytes 147460
  160.5 4.3 %copy-start.4 = (bf16[16,1344]{1,0:T(8,128)(2,1)S(1)}, bf16[16,1344]{1,0:T(8,128)(2,1)}, u32[]{:S(2)}) copy-start(bf16[16,1344]{1,0:T(8,128)(2,1)} %param.19) | copy-start | bytes 129028
  160.5 40.1 %all-to-all-start.1 = ((bf16[2,8,2,64,768]{4,3,1,2,0:T(8,128)(2,1)}), bf16[2,8,2,64,768]{4,3,1,2,0:T(8,128)(2,1)S(1)}, u32[]{:S(2)}, u32[]{:S(2)}) async-start(bf16[2,8,2,64,768]{4,3,1,2,0:T(8,128)(2,1)} %pad_maximum_fusion), calls=%async_computation.1 | async-start | bytes 6291456 | tf_op jit(solution)/shard_map/all_to_all | solution.py:57
  212.7 4.0 %copy-start.1 = (f32[128,6]{0,1:T(8,128)S(1)}, f32[128,6]{0,1:T(8,128)}, u32[]{:S(2)}) copy-start(f32[128,6]{0,1:T(8,128)} %param.12) | copy-start | bytes 9220
  212.7 69.6 %all-to-all-start.2 = ((bf16[8,2,64,1344]{3,2,1,0:T(8,128)(2,1)}), bf16[8,2,64,1344]{3,2,1,0:T(8,128)(2,1)S(1)}, u32[]{:S(2)}, u32[]{:S(2)}) async-start(bf16[8,2,64,1344]{3,2,1,0:T(8,128)(2,1)} %copy.38), calls=%async_computation.2 | async-start | bytes 5767168 | tf_op jit(solution)/shard_map/all_to_all | solution.py:68
